TPU v7x, 32 devices: a whole 2x2x4 slice. The times are simulated.
32 devices in a mesh: grp: 2 (over x), wide: 16 (over z, y, core).
Axes of the slice: x: 2, y: 2, z: 4, core: 2. Of those that a mesh axis runs over, the one named last changes fastest.
Arguments:
- queries: bfloat16 [256, 4096], P(('grp', 'wide')), parts along dimension 0, may hold values from -8 to 8
- draft_keys: bfloat16 [256, 512], P(('grp', 'wide')), parts along dimension 0, may hold values from -8 to 8
- draft_values: bfloat16 [256, 512], P(('grp', 'wide')), parts along dimension 0, may hold values from -24 to 24
- cache_keys: bfloat16 [262144, 128], P(('grp', 'wide')), parts along dimension 0, may hold values from -8 to 8
- cache_values: bfloat16 [262144, 128], P(('grp', 'wide')), parts along dimension 0, may hold values from -24 to 24
- block_owner: int32 [32], P('grp'), parts along dimension 0, may hold values from 0 to 15, each once
- block_lengths: int32 [32], P('grp'), parts along dimension 0, may hold values from 1024 to 8192, as said below
- draft_mask: int32 [4, 64, 64], P('grp'), parts along dimension 0, may hold values from 0 to 1, as said below
- out_weight: bfloat16 [4096, 8192], P(None, 'wide'), may hold values from -1 to 1
- norm_gain: float32 [8192], replicated, may hold values from 0.25 to 1.75
- gate_weight: bfloat16 [8192, 14336], P(None, 'wide'), may hold values from -0.0625 to 0.0625
- up_weight: bfloat16 [8192, 14336], P(None, 'wide'), may hold values from -0.0625 to 0.0625
Outputs:
- projected: bfloat16 [256, 8192], P('grp', 'wide'), parts along dimension 0
- hidden: bfloat16 [256, 14336], P('grp', 'wide'), parts along dimension 0
There are 2 independent parts, one for each index of `grp`. A program takes and returns all parts, laid end to end along the dimension named above; an argument that names none is the same for every part. Nothing has to cross between parts.
Inputs may be any that keep to these rules, and one draw needn't show every extreme that they name: `block_owner`: each device holds exactly one block. `block_lengths`: at most 8192 rows a block, and some block has exactly 8192 rows. In each sequence row 0 is the root of a tree in which every other row's parent lies 1 to 4 rows before it; draft_mask[s, i, t] is 1 exactly when t is i or an ancestor of i.
All inputs are finite; a program needn't handle non-finite values.
Results may differ from a plain program's by a relative error of at most 0.02.
Values may be sent and summed in bfloat16 or wider, within the bound.
A program may use at most 128 MiB of HBM per device.

v0:
```python
import math
import jax
import jax.numpy as jnp
from jax import lax
from jax.sharding import PartitionSpec as P

very_low = -1e30
epsilon = 1e-05


def block_update(state, query_rows, block_keys, block_values, valid, scale):
    running, total, weighted = state
    scores = (
        jnp.einsum("igc,kc->igk", query_rows, block_keys, preferred_element_type=jnp.float32)
        * scale
    )
    scores = jnp.where(valid, scores, very_low)
    newest = jnp.maximum(running, jnp.max(scores, axis=-1))
    factor = jnp.exp(running - newest)
    weights = jnp.where(valid, jnp.exp(scores - newest[..., None]), 0.0)
    total = total * factor + jnp.sum(weights, axis=-1)
    weighted = weighted * factor[..., None] + jnp.einsum(
        "igk,kc->igc",
        weights.astype(jnp.bfloat16),
        block_values,
        preferred_element_type=jnp.float32,
    )
    return (newest, total, weighted)


def attend(query_rows, keys, values, length, own_keys, own_values, own_valid):
    block_size = min(512, keys.shape[0])
    scale = 1.0 / math.sqrt(query_rows.shape[2])
    rows_count = query_rows.shape[0]
    heads = query_rows.shape[1]
    state = (
        jnp.full((rows_count, heads), very_low, jnp.float32),
        jnp.zeros((rows_count, heads), jnp.float32),
        jnp.zeros((rows_count, heads, query_rows.shape[2]), jnp.float32),
    )
    offsets = jnp.arange(block_size, dtype=jnp.int32)

    def advance(number, carry):
        begin = (number * block_size).astype(jnp.int32)
        block_keys = lax.dynamic_slice_in_dim(keys, begin, block_size, 0)
        block_values = lax.dynamic_slice_in_dim(values, begin, block_size, 0)
        valid = (begin + offsets < length)[None, None, :]
        return block_update(carry, query_rows, block_keys, block_values, valid, scale)

    count = (length + block_size - 1) // block_size
    state = lax.fori_loop(jnp.int32(0), count, advance, state)
    return block_update(state, query_rows, own_keys, own_values, own_valid[:, None, :], scale)


def per_device(
    queries,
    draft_keys,
    draft_values,
    cache_keys,
    cache_values,
    block_owner,
    block_lengths,
    draft_mask,
    out_weight,
    norm_gain,
    gate_weight,
    up_weight,
):
    devices = lax.axis_size("wide")
    own_index = lax.axis_index("wide")
    head_size = cache_keys.shape[1]
    key_heads = draft_keys.shape[1] // head_size
    group_width = queries.shape[1] // key_heads
    group = group_width // head_size
    sequences = draft_mask.shape[0]
    draft_rows = draft_mask.shape[1]
    all_rows = sequences * draft_rows
    local_rows = queries.shape[0]
    heads_all = key_heads * group
    blocks_per_pair = devices // (sequences * key_heads)
    device_ids = jnp.arange(devices, dtype=jnp.int32)
    owned = (block_owner[None, :] == device_ids[:, None]).astype(jnp.int32)
    device_block = jnp.sum(owned * device_ids[None, :], axis=1)
    device_pair = device_block // blocks_per_pair
    device_sequence = device_pair // key_heads
    device_head = device_pair % key_heads
    device_length = jnp.sum(owned * block_lengths[None, :], axis=1)
    picker = (device_ids == own_index).astype(jnp.int32)
    own_block = jnp.sum(picker * device_block)
    own_sequence = jnp.sum(picker * device_sequence)
    own_head = jnp.sum(picker * device_head)
    own_length = jnp.sum(picker * device_length)
    is_last = own_block % blocks_per_pair == blocks_per_pair - 1
    row_start = own_sequence * draft_rows
    head_numbers = jnp.arange(key_heads, dtype=jnp.int32)
    every_query, every_key, every_value = (
        lax.all_gather(queries, "wide", axis=0, tiled=True),
        lax.all_gather(draft_keys, "wide", axis=0, tiled=True),
        lax.all_gather(draft_values, "wide", axis=0, tiled=True),
    )
    query_columns = own_head * group_width
    key_columns = own_head * head_size
    pair_queries = lax.dynamic_slice_in_dim(
        lax.dynamic_slice_in_dim(every_query, row_start, draft_rows, 0),
        query_columns,
        group_width,
        1,
    )
    pair_keys = lax.dynamic_slice_in_dim(
        lax.dynamic_slice_in_dim(every_key, row_start, draft_rows, 0), key_columns, head_size, 1
    )
    pair_values = lax.dynamic_slice_in_dim(
        lax.dynamic_slice_in_dim(every_value, row_start, draft_rows, 0), key_columns, head_size, 1
    )
    own_head = jnp.sum(picker * device_head)
    query_rows = pair_queries.reshape(draft_rows, group, head_size)
    own_valid = (
        lax.dynamic_index_in_dim(draft_mask, own_sequence, 0, keepdims=False) > 0
    ) & is_last
    running, total, weighted = attend(
        query_rows, cache_keys, cache_values, own_length, pair_keys, pair_values, own_valid
    )
    block_output = (weighted / total[..., None]).astype(jnp.bfloat16)
    slot_peak = lax.dynamic_update_slice(
        jnp.full((all_rows, group), very_low, jnp.float32), running, (row_start, jnp.int32(0))
    ).reshape(devices, local_rows, group)
    slot_total = lax.dynamic_update_slice(
        jnp.zeros((all_rows, group), jnp.float32), total, (row_start, jnp.int32(0))
    ).reshape(devices, local_rows, group)
    slot_output = lax.dynamic_update_slice(
        jnp.zeros((all_rows, group, head_size), jnp.bfloat16),
        block_output,
        (row_start, jnp.int32(0), jnp.int32(0)),
    ).reshape(devices, local_rows, group, head_size)
    back_peak, back_total = (
        lax.all_to_all(slot_peak, "wide", split_axis=0, concat_axis=0, tiled=True),
        lax.all_to_all(slot_total, "wide", split_axis=0, concat_axis=0, tiled=True),
    )
    back_output = lax.all_to_all(slot_output, "wide", split_axis=0, concat_axis=0, tiled=True)
    member = device_head[:, None] == head_numbers[None, :]
    spread = jnp.where(member[:, None, :, None], back_peak[:, :, None, :], very_low)
    highest = jnp.max(spread, axis=0)
    mixing = jnp.exp(spread - highest[None]) * back_total[:, :, None, :]
    row_total = jnp.sum(mixing, axis=0)
    row_weighted = jnp.einsum(
        "srgj,srjc->rgjc", mixing, back_output.astype(jnp.float32), precision=lax.Precision.HIGHEST
    )
    attended_rows = (
        (row_weighted / row_total[..., None])
        .astype(jnp.bfloat16)
        .reshape(local_rows, heads_all * head_size)
    )
    combined = jnp.dot(
        lax.all_gather(attended_rows, "wide", axis=0, tiled=True),
        out_weight,
        preferred_element_type=jnp.float32,
    )
    projected = combined.astype(jnp.bfloat16)
    columns = projected.shape[1]
    branch = lax.optimization_barrier(projected).astype(jnp.float32)
    squares = lax.psum(jnp.sum(branch * branch, axis=1), "wide")
    inverse = lax.rsqrt(squares / (columns * devices) + epsilon)
    gain_part = lax.dynamic_slice_in_dim(norm_gain, own_index * columns, columns, 0)
    normed = (branch * inverse[:, None] * gain_part[None, :]).astype(jnp.bfloat16)
    piece = lax.all_gather(normed, "wide", axis=1, tiled=True)
    gate = jnp.dot(piece, gate_weight, preferred_element_type=jnp.float32)
    upward = jnp.dot(piece, up_weight, preferred_element_type=jnp.float32)
    hidden = (jax.nn.silu(gate) * upward).astype(jnp.bfloat16)
    return (projected, hidden)


def solution(mesh):
    placed = (
        P(("grp", "wide"), None),
        P(("grp", "wide"), None),
        P(("grp", "wide"), None),
        P(("grp", "wide"), None),
        P(("grp", "wide"), None),
        P("grp"),
        P("grp"),
        P("grp", None, None),
        P(None, "wide"),
        P(),
        P(None, "wide"),
        P(None, "wide"),
    )
    return jax.shard_map(
        per_device,
        mesh=mesh,
        in_specs=placed,
        out_specs=(P("grp", "wide"), P("grp", "wide")),
        check_vma=False,
    )
```

profile of v0, /device:TPU:0, one launch (start us, length us, event | category | flops | bytes accessed | tf_op | source)
XLA Modules:
  0.0 300.9 jit_solution(8862913507777741700)
XLA Ops:
  7.9 0.8 select_reduce_fusion.2
  16.7 23.9 %all_gather.16 = bf16[128,512]{1,0:T(8,128)(2,1)S(1)} all-gather(bf16[8,512]{1,0:T(8,128)(2,1)} %param.15), channel_id=1, replica_groups=mesh['grp'=2,'wide'=16] {'wide'}, dimensions={0}, use_global_device_ids=true | all-gather | bytes 139264 | tf_op jit(solution)/shard_map/all_gather | solution.py:98
  41.4 9.5 %all-gather.4.cloned.1.call-done = bf16[128,4096]{1,0:T(8,128)(2,1)} async-done(((bf16[8,4096]{1,0:T(8,128)(2,1)}), bf16[128,4096]{1,0:T(8,128)(2,1)}) %all-gather.4.cloned.1.call-update) | async-done | bytes 1048592 | tf_op jit(solution)/shard_map/all_gather | solution.py:97
  50.9 1.0 dynamic-slice_bitcast_fusion.1
  52.5 11.5 %while.15 = (s32[]{:T(128)}, f32[64,8]{0,1:T(8,128)S(1)}, f32[64,8]{0,1:T(8,128)S(1)}, f32[64,8,128]{2,1,0:T(8,128)S(1)}, s32[]{:T(128)}, /*index=5*/s32[]{:T(12...) while((s32[]{:T(128)}, f32[64,8]{0,1:T(8,128)S(1)}, ...), condition=%wide.region_8.9_spmd.clone, body=%wide.region_5.8_spmd.clone.sunk | while | flops 136185856 | bytes 4099771 | solution.py:51
  53.3 1.3 fusion.69
  55.0 1.3 convolution_add_fusion.3
  57.1 1.3 fusion.69
  58.9 1.3 convolution_add_fusion.3
  60.9 1.3 fusion.69
  62.7 1.3 convolution_add_fusion.3
  65.5 52.4 %all-to-all-start.2 = ((f32[16,8,8]{1,2,0:T(8,128)}), f32[16,8,8]{1,2,0:T(8,128)S(1)}, u32[]{:S(2)}, u32[]{:S(2)}) async-start(f32[16,8,8]{1,2,0:T(8,128)} %copy.68), calls=%async_computation.2 | async-start | bytes 131072 | tf_op jit(solution)/shard_map/all_to_all | solution.py:137
  117.9 22.1 %all_gather.17 = bf16[128,512]{1,0:T(8,128)(2,1)S(1)} all-gather(bf16[8,512]{1,0:T(8,128)(2,1)S(1)} %copy-done.2), channel_id=1, replica_groups=mesh['grp'=2,'wide'=16] {'wide'}, dimensions={0}, use_global_device_ids=true | all-gather | bytes 139264 | tf_op jit(solution)/shard_map/all_gather | solution.py:99
  141.1 3.5 %all-to-all-start.1 = ((f32[16,8,8]{1,2,0:T(8,128)}), f32[16,8,8]{1,2,0:T(8,128)S(1)}, u32[]{:S(2)}, u32[]{:S(2)}) async-start(f32[16,8,8]{1,2,0:T(8,128)} %copy.66), calls=%async_computation.1 | async-start | bytes 131072 | tf_op jit(solution)/shard_map/all_to_all | solution.py:136
  145.4 0.9 fusion.18
  146.3 5.2 %all-to-all-done.1 = f32[16,8,8]{1,2,0:T(8,128)S(1)} async-done(((f32[16,8,8]{1,2,0:T(8,128)}), f32[16,8,8]{1,2,0:T(8,128)S(1)}, u32[]{:S(2)}, u32[]{:S(2)}) %all-to-all-start.1) | async-done | bytes 4128 | tf_op jit(solution)/shard_map/all_to_all | solution.py:136
  151.5 3.5 %all-to-all-start = ((bf16[16,8,8,128]{3,2,1,0:T(8,128)(2,1)}), bf16[16,8,8,128]{3,2,1,0:T(8,128)(2,1)S(1)}, u32[]{:S(2)}, u32[]{:S(2)}) async-start(bf16[16,8,8,128]{3,2,1,0:T(8,128)(2,1)} %bitcast.3), calls=%async_computation | async-start | bytes 524288 | tf_op jit(solution)/shard_map/all_to_all | solution.py:139
  155.7 9.3 %all-to-all-done = bf16[16,8,8,128]{3,2,1,0:T(8,128)(2,1)S(1)} async-done(((bf16[16,8,8,128]{3,2,1,0:T(8,128)(2,1)}), bf16[16,8,8,128]{3,2,1,0:T(8,128)(2,1)S(1)}, u32[]{:S(2)}, u32[]{:S(2)}) %all-to-all-start) | async-done | bytes 262176 | tf_op jit(solution)/shard_map/all_to_all | solution.py:139
  167.1 36.5 %all-gather.6.cloned.1.call-done = bf16[128,4096]{1,0:T(8,128)(2,1)} async-done(((bf16[8,4096]{1,0:T(8,128)(2,1)}), bf16[128,4096]{1,0:T(8,128)(2,1)}) %all-gather.6.cloned.1.call-update) | async-done | bytes 1048592 | tf_op jit(solution)/shard_map/all_gather | solution.py:154
  203.5 3.2 %convolution_convert_fusion = bf16[128,512]{1,0:T(8,128)(2,1)S(1)} fusion(bf16[128,4096]{1,0:T(8,128)(2,1)} %all-gather.6.cloned.1.call-done, bf16[4096,512]{1,0:T(8,128)(2,1)} %param.22), kind=kOutput, calls=%fused_computation.27 | convolution fusion | flops 536936448 | bytes 5373952 | tf_op jit(solution)/shard_map/dot_general | solution.py:153
  206.9 31.6 %psum.7 = f32[128]{0:T(128)S(1)} all-reduce(f32[128]{0:T(128)S(1)} %fusion.21), channel_id=1, replica_groups=mesh['grp'=2,'wide'=16] {'wide'}, use_global_device_ids=true, to_apply=%region_15.16 | all-reduce | flops 128 | bytes 1024 | tf_op jit(solution)/shard_map/psum | solution.py:161
  239.3 38.4 %all-gather.8.cloned.1.call-done = bf16[128,8192]{1,0:T(8,128)(2,1)} async-done(((bf16[128,512]{1,0:T(8,128)(2,1)}), bf16[128,8192]{1,0:T(8,128)(2,1)}) %all-gather.8.cloned.1.call-update) | async-done | bytes 2097168 | tf_op jit(solution)/shard_map/all_gather | solution.py:165
  277.7 8.3 %fusion.50 = f32[128,896]{1,0:T(8,128)S(1)} fusion(bf16[128,8192]{1,0:T(8,128)(2,1)} %all-gather.8.cloned.1.call-done, bf16[8192,896]{1,0:T(8,128)(2,1)} %param.24), kind=kOutput, calls=%fused_computation.90 | convolution fusion | flops 1879048192 | bytes 17235968 | tf_op jit(solution)/shard_map/dot_general | solution.py:166
  286.1 8.3 %fusion.14 = bf16[128,896]{1,0:T(8,128)(2,1)} fusion(bf16[128,8192]{1,0:T(8,128)(2,1)S(1)} %copy-done, bf16[8192,896]{1,0:T(8,128)(2,1)} %param.25, f32[128,896]{1,0:T(8,128)S(1)} %fusion.50), kind=kOutput, calls=%fused_computation.20 | convolution fusion | flops 1879736320 | bytes 17465344 | tf_op jit(solution)/shard_map/dot_general | solution.py:167
  (69 shorter events, 13.8 us)
Async XLA Ops:
  7.2 43.8 %all-gather.4.cloned.1.call-start = ((), (), s32[]{:S(2)}) async-start(), calls=%async_computation.3 | async-start | bytes 1114112 | tf_op jit(solution)/shard_map/all_gather | solution.py:97
  52.5 65.3 %copy-start.2 = (bf16[8,512]{1,0:T(8,128)(2,1)S(1)}, bf16[8,512]{1,0:T(8,128)(2,1)}, u32[]{:S(2)}) copy-start(bf16[8,512]{1,0:T(8,128)(2,1)} %param.16) | copy-start | bytes 24580
  65.5 75.7 %all-to-all-start.2 = ((f32[16,8,8]{1,2,0:T(8,128)}), f32[16,8,8]{1,2,0:T(8,128)S(1)}, u32[]{:S(2)}, u32[]{:S(2)}) async-start(f32[16,8,8]{1,2,0:T(8,128)} %copy.68), calls=%async_computation.2 | async-start | bytes 131072 | tf_op jit(solution)/shard_map/all_to_all | solution.py:137
  141.1 10.4 %all-to-all-start.1 = ((f32[16,8,8]{1,2,0:T(8,128)}), f32[16,8,8]{1,2,0:T(8,128)S(1)}, u32[]{:S(2)}, u32[]{:S(2)}) async-start(f32[16,8,8]{1,2,0:T(8,128)} %copy.66), calls=%async_computation.1 | async-start | bytes 131072 | tf_op jit(solution)/shard_map/all_to_all | solution.py:136
  151.5 13.5 %all-to-all-start = ((bf16[16,8,8,128]{3,2,1,0:T(8,128)(2,1)}), bf16[16,8,8,128]{3,2,1,0:T(8,128)(2,1)S(1)}, u32[]{:S(2)}, u32[]{:S(2)}) async-start(bf16[16,8,8,128]{3,2,1,0:T(8,128)(2,1)} %bitcast.3), calls=%async_computation | async-start | bytes 524288 | tf_op jit(solution)/shard_map/all_to_all | solution.py:139
  155.0 48.5 %all-gather.6.cloned.1.call-start = ((), (), s32[]{:S(2)}) async-start(), calls=%async_computation.4 | async-start | bytes 1114112 | tf_op jit(solution)/shard_map/all_gather | solution.py:154
  166.3 111.5 %all-gather.8.cloned.1.call-start = ((), (), s32[]{:S(2)}) async-start(), calls=%async_computation.5 | async-start | bytes 2228224 | tf_op jit(solution)/shard_map/all_gather | solution.py:165
  206.8 79.3 %copy-start.1 = (bf16[128,512]{1,0:T(8,128)(2,1)}, bf16[128,512]{1,0:T(8,128)(2,1)S(1)}, u32[]{:S(2)}) copy-start(bf16[128,512]{1,0:T(8,128)(2,1)S(1)} %convolution_convert_fusion) | copy-start | bytes 393220
  277.7 8.3 %copy-start = (bf16[128,8192]{1,0:T(8,128)(2,1)S(1)}, bf16[128,8192]{1,0:T(8,128)(2,1)}, u32[]{:S(2)}) copy-start(bf16[128,8192]{1,0:T(8,128)(2,1)} %all-gather.8.cloned.1.call-done) | copy-start | bytes 6291460
Sparse Core Ops, SparseCore 0:
  10.1 40.7 all-gather.3
  166.4 37.1 all-gather.5
  239.4 38.2 all-gather.7
where the time goes:
time: 302 us; the launch traced here: 301 us
  waiting for transfers between devices  99.6 us (33%)
  blocking collectives  77.6 us (26%)
  starting transfers between devices  59.5 us (20%)
  matrix products  29.6 us (10%)
  between operations  20.6 us (7%)
  other arithmetic  7.69 us (3%)
  local copies, waits for them, and re-layouts  6.13 us (2%)
    all_to_all x1, starting transfers between devices, per_device(): lax.all_to_all(slot_total, 'wide', split_axis=0, concat_axis=0, tiled=True)  52.4 us
    all_gather x1, waiting for transfers between devices, per_device(): piece = lax.all_gather(normed, 'wide', axis=1, tiled=True)  38.4 us
    all_gather x1, waiting for transfers between devices, per_device(): lax.all_gather(attended_rows, 'wide', axis=0, tiled=True)  36.5 us
    psum x1, blocking collectives, per_device(): squares = lax.psum(jnp.sum(branch * branch, axis=1), 'wide')  31.6 us
    all_gather x1, blocking collectives, per_device(): lax.all_gather(draft_keys, 'wide', axis=0, tiled=True)  23.9 us
    all_gather x1, blocking collectives, per_device(): lax.all_gather(draft_values, 'wide', axis=0, tiled=True)  22.1 us
    all_gather x1, waiting for transfers between devices, per_device(): lax.all_gather(queries, 'wide', axis=0, tiled=True)  9.54 us
    all_to_all x1, waiting for transfers between devices, per_device(): lax.all_to_all(slot_output, 'wide', split_axis=0, concat_axis=0, tiled=True)  9.29 us
  transfers between devices with their start and end apart: 6, of which 5 were waited for; matrix products, arithmetic and copies ran while one was open for 2% of the time, Pallas kernels for 0%

commit v1 on v0

--- a/solution.py
+++ b/solution.py
@@ -158,7 +158,9 @@
     projected = combined.astype(jnp.bfloat16)
     columns = projected.shape[1]
     branch = lax.optimization_barrier(projected).astype(jnp.float32)
-    squares = lax.psum(jnp.sum(branch * branch, axis=1), "wide")
+    own = jnp.sum(branch * branch, axis=1)
+    parts = lax.all_gather(own, "wide", axis=0, tiled=False)
+    squares = parts.sum(axis=0)
     inverse = lax.rsqrt(squares / (columns * devices) + epsilon)
     gain_part = lax.dynamic_slice_in_dim(norm_gain, own_index * columns, columns, 0)
     normed = (branch * inverse[:, None] * gain_part[None, :]).astype(jnp.bfloat16)

time: 302 us -> 290 us (0.960)
  blocking collectives: 77.6 us -> 65.4 us
    psum x1 -> x0, blocking collectives: 31.6 us -> none  [per_device(): squares = lax.psum(jnp.sum(branch * branch, axis=1), 'wide')]
    all_gather x0 -> x1, blocking collectives: none -> 19.4 us  [per_device(): parts = lax.all_gather(own, 'wide', axis=0, tiled=False)]
where the time goes in v1:
time: 290 us; the launch traced here: 289 us
  waiting for transfers between devices  99.6 us (34%)
  blocking collectives  65.4 us (23%)
  starting transfers between devices  59.5 us (21%)
  matrix products  29.6 us (10%)
  between operations  20.6 us (7%)
  other arithmetic  7.72 us (3%)
  local copies, waits for them, and re-layouts  6.13 us (2%)
    all_to_all x1, starting transfers between devices, per_device(): lax.all_to_all(slot_total, 'wide', split_axis=0, concat_axis=0, tiled=True)  52.4 us
    all_gather x1, waiting for transfers between devices, per_device(): piece = lax.all_gather(normed, 'wide', axis=1, tiled=True)  38.4 us
    all_gather x1, waiting for transfers between devices, per_device(): lax.all_gather(attended_rows, 'wide', axis=0, tiled=True)  36.5 us
    all_gather x1, blocking collectives, per_device(): lax.all_gather(draft_keys, 'wide', axis=0, tiled=True)  23.9 us
    all_gather x1, blocking collectives, per_device(): lax.all_gather(draft_values, 'wide', axis=0, tiled=True)  22.1 us
    all_gather x1, blocking collectives, per_device(): parts = lax.all_gather(own, 'wide', axis=0, tiled=False)  19.4 us
    all_gather x1, waiting for transfers between devices, per_device(): lax.all_gather(queries, 'wide', axis=0, tiled=True)  9.54 us
    all_to_all x1, waiting for transfers between devices, per_device(): lax.all_to_all(slot_output, 'wide', split_axis=0, concat_axis=0, tiled=True)  9.29 us
  transfers between devices with their start and end apart: 6, of which 5 were waited for; matrix products, arithmetic and copies ran while one was open for 2% of the time, Pallas kernels for 0%

profile of v1, /device:TPU:0, one launch (start us, length us, event | category | flops | bytes accessed | tf_op | source)
XLA Modules:
  0.0 288.7 jit_solution(1832700702973865646)
XLA Ops:
  7.9 0.8 select_reduce_fusion.2
  16.7 23.9 %all_gather.22 = bf16[128,512]{1,0:T(8,128)(2,1)S(1)} all-gather(bf16[8,512]{1,0:T(8,128)(2,1)} %param.15), channel_id=1, replica_groups=mesh['grp'=2,'wide'=16] {'wide'}, dimensions={0}, use_global_device_ids=true | all-gather | bytes 139264 | tf_op jit(solution)/shard_map/all_gather | solution.py:98
  41.4 9.5 %all-gather.6.cloned.1.call-done = bf16[128,4096]{1,0:T(8,128)(2,1)} async-done(((bf16[8,4096]{1,0:T(8,128)(2,1)}), bf16[128,4096]{1,0:T(8,128)(2,1)}) %all-gather.6.cloned.1.call-update) | async-done | bytes 1048592 | tf_op jit(solution)/shard_map/all_gather | solution.py:97
  50.9 1.0 dynamic-slice_bitcast_fusion.1
  52.5 11.5 %while.15 = (s32[]{:T(128)}, f32[64,8]{0,1:T(8,128)S(1)}, f32[64,8]{0,1:T(8,128)S(1)}, f32[64,8,128]{2,1,0:T(8,128)S(1)}, s32[]{:T(128)}, /*index=5*/s32[]{:T(12...) while((s32[]{:T(128)}, f32[64,8]{0,1:T(8,128)S(1)}, ...), condition=%wide.region_8.9_spmd.clone, body=%wide.region_5.8_spmd.clone.sunk | while | flops 136185856 | bytes 4099771 | solution.py:51
  53.3 1.3 fusion.69
  55.0 1.3 convolution_add_fusion.3
  57.1 1.3 fusion.69
  58.9 1.3 convolution_add_fusion.3
  60.9 1.3 fusion.69
  62.7 1.3 convolution_add_fusion.3
  65.5 52.4 %all-to-all-start.2 = ((f32[16,8,8]{1,2,0:T(8,128)}), f32[16,8,8]{1,2,0:T(8,128)S(1)}, u32[]{:S(2)}, u32[]{:S(2)}) async-start(f32[16,8,8]{1,2,0:T(8,128)} %copy.68), calls=%async_computation.2 | async-start | bytes 131072 | tf_op jit(solution)/shard_map/all_to_all | solution.py:137
  117.9 22.1 %all_gather.23 = bf16[128,512]{1,0:T(8,128)(2,1)S(1)} all-gather(bf16[8,512]{1,0:T(8,128)(2,1)S(1)} %copy-done.2), channel_id=1, replica_groups=mesh['grp'=2,'wide'=16] {'wide'}, dimensions={0}, use_global_device_ids=true | all-gather | bytes 139264 | tf_op jit(solution)/shard_map/all_gather | solution.py:99
  141.1 3.5 %all-to-all-start.1 = ((f32[16,8,8]{1,2,0:T(8,128)}), f32[16,8,8]{1,2,0:T(8,128)S(1)}, u32[]{:S(2)}, u32[]{:S(2)}) async-start(f32[16,8,8]{1,2,0:T(8,128)} %copy.66), calls=%async_computation.1 | async-start | bytes 131072 | tf_op jit(solution)/shard_map/all_to_all | solution.py:136
  145.4 0.9 fusion.18
  146.3 5.2 %all-to-all-done.1 = f32[16,8,8]{1,2,0:T(8,128)S(1)} async-done(((f32[16,8,8]{1,2,0:T(8,128)}), f32[16,8,8]{1,2,0:T(8,128)S(1)}, u32[]{:S(2)}, u32[]{:S(2)}) %all-to-all-start.1) | async-done | bytes 4128 | tf_op jit(solution)/shard_map/all_to_all | solution.py:136
  151.5 3.5 %all-to-all-start = ((bf16[16,8,8,128]{3,2,1,0:T(8,128)(2,1)}), bf16[16,8,8,128]{3,2,1,0:T(8,128)(2,1)S(1)}, u32[]{:S(2)}, u32[]{:S(2)}) async-start(bf16[16,8,8,128]{3,2,1,0:T(8,128)(2,1)} %bitcast.3), calls=%async_computation | async-start | bytes 524288 | tf_op jit(solution)/shard_map/all_to_all | solution.py:139
  155.7 9.3 %all-to-all-done = bf16[16,8,8,128]{3,2,1,0:T(8,128)(2,1)S(1)} async-done(((bf16[16,8,8,128]{3,2,1,0:T(8,128)(2,1)}), bf16[16,8,8,128]{3,2,1,0:T(8,128)(2,1)S(1)}, u32[]{:S(2)}, u32[]{:S(2)}) %all-to-all-start) | async-done | bytes 262176 | tf_op jit(solution)/shard_map/all_to_all | solution.py:139
  167.1 36.5 %all-gather.8.cloned.1.call-done = bf16[128,4096]{1,0:T(8,128)(2,1)} async-done(((bf16[8,4096]{1,0:T(8,128)(2,1)}), bf16[128,4096]{1,0:T(8,128)(2,1)}) %all-gather.8.cloned.1.call-update) | async-done | bytes 1048592 | tf_op jit(solution)/shard_map/all_gather | solution.py:154
  203.5 3.2 %convolution_convert_fusion = bf16[128,512]{1,0:T(8,128)(2,1)S(1)} fusion(bf16[128,4096]{1,0:T(8,128)(2,1)} %all-gather.8.cloned.1.call-done, bf16[4096,512]{1,0:T(8,128)(2,1)} %param.22), kind=kOutput, calls=%fused_computation.27 | convolution fusion | flops 536936448 | bytes 5373952 | tf_op jit(solution)/shard_map/dot_general | solution.py:153
  206.9 19.4 %all-gather.1 = f32[16,1,128]{2,1,0:T(1,128)S(1)} all-gather(f32[1,1,128]{2,1,0:T(1,128)S(1)} %bitcast.65), channel_id=2, replica_groups=mesh['grp'=2,'wide'=16] {'wide'}, dimensions={0}, use_global_device_ids=true | all-gather | bytes 8704 | tf_op jit(solution)/shard_map/all_gather | solution.py:162
  227.1 38.4 %all-gather.10.cloned.1.call-done = bf16[128,8192]{1,0:T(8,128)(2,1)} async-done(((bf16[128,512]{1,0:T(8,128)(2,1)}), bf16[128,8192]{1,0:T(8,128)(2,1)}) %all-gather.10.cloned.1.call-update) | async-done | bytes 2097168 | tf_op jit(solution)/shard_map/all_gather | solution.py:167
  265.6 8.3 %fusion.50 = f32[128,896]{1,0:T(8,128)S(1)} fusion(bf16[128,8192]{1,0:T(8,128)(2,1)} %all-gather.10.cloned.1.call-done, bf16[8192,896]{1,0:T(8,128)(2,1)} %param.24), kind=kOutput, calls=%fused_computation.90 | convolution fusion | flops 1879048192 | bytes 17235968 | tf_op jit(solution)/shard_map/dot_general | solution.py:168
  273.9 8.3 %fusion.14 = bf16[128,896]{1,0:T(8,128)(2,1)} fusion(bf16[128,8192]{1,0:T(8,128)(2,1)S(1)} %copy-done, bf16[8192,896]{1,0:T(8,128)(2,1)} %param.25, f32[128,896]{1,0:T(8,128)S(1)} %fusion.50), kind=kOutput, calls=%fused_computation.20 | convolution fusion | flops 1879736320 | bytes 17465344 | tf_op jit(solution)/shard_map/dot_general | solution.py:169
  (70 shorter events, 13.8 us)
Async XLA Ops:
  7.2 43.8 %all-gather.6.cloned.1.call-start = ((), (), s32[]{:S(2)}) async-start(), calls=%async_computation.3 | async-start | bytes 1114112 | tf_op jit(solution)/shard_map/all_gather | solution.py:97
  52.5 65.3 %copy-start.2 = (bf16[8,512]{1,0:T(8,128)(2,1)S(1)}, bf16[8,512]{1,0:T(8,128)(2,1)}, u32[]{:S(2)}) copy-start(bf16[8,512]{1,0:T(8,128)(2,1)} %param.16) | copy-start | bytes 24580
  65.5 75.7 %all-to-all-start.2 = ((f32[16,8,8]{1,2,0:T(8,128)}), f32[16,8,8]{1,2,0:T(8,128)S(1)}, u32[]{:S(2)}, u32[]{:S(2)}) async-start(f32[16,8,8]{1,2,0:T(8,128)} %copy.68), calls=%async_computation.2 | async-start | bytes 131072 | tf_op jit(solution)/shard_map/all_to_all | solution.py:137
  141.1 10.4 %all-to-all-start.1 = ((f32[16,8,8]{1,2,0:T(8,128)}), f32[16,8,8]{1,2,0:T(8,128)S(1)}, u32[]{:S(2)}, u32[]{:S(2)}) async-start(f32[16,8,8]{1,2,0:T(8,128)} %copy.66), calls=%async_computation.1 | async-start | bytes 131072 | tf_op jit(solution)/shard_map/all_to_all | solution.py:136
  151.5 13.5 %all-to-all-start = ((bf16[16,8,8,128]{3,2,1,0:T(8,128)(2,1)}), bf16[16,8,8,128]{3,2,1,0:T(8,128)(2,1)S(1)}, u32[]{:S(2)}, u32[]{:S(2)}) async-start(bf16[16,8,8,128]{3,2,1,0:T(8,128)(2,1)} %bitcast.3), calls=%async_computation | async-start | bytes 524288 | tf_op jit(solution)/shard_map/all_to_all | solution.py:139
  155.0 48.5 %all-gather.8.cloned.1.call-start = ((), (), s32[]{:S(2)}) async-start(), calls=%async_computation.4 | async-start | bytes 1114112 | tf_op jit(solution)/shard_map/all_gather | solution.py:154
  166.3 99.3 %all-gather.10.cloned.1.call-start = ((), (), s32[]{:S(2)}) async-start(), calls=%async_computation.5 | async-start | bytes 2228224 | tf_op jit(solution)/shard_map/all_gather | solution.py:167
  206.8 67.1 %copy-start.1 = (bf16[128,512]{1,0:T(8,128)(2,1)}, bf16[128,512]{1,0:T(8,128)(2,1)S(1)}, u32[]{:S(2)}) copy-start(bf16[128,512]{1,0:T(8,128)(2,1)S(1)} %convolution_convert_fusion) | copy-start | bytes 393220
  265.6 8.3 %copy-start = (bf16[128,8192]{1,0:T(8,128)(2,1)S(1)}, bf16[128,8192]{1,0:T(8,128)(2,1)}, u32[]{:S(2)}) copy-start(bf16[128,8192]{1,0:T(8,128)(2,1)} %all-gather.10.cloned.1.call-done) | copy-start | bytes 6291460
Sparse Core Ops, SparseCore 0:
  10.1 40.7 all-gather.5
  166.4 37.1 all-gather.7
  227.3 38.2 all-gather.9
